TPU v7x, 32 devices: a whole 2x2x4 slice. The times are simulated.
32 devices in a mesh: row: 8 (over y, x, core), col: 4 (over z).
Axes of the slice: x: 2, y: 2, z: 4, core: 2. Of those that a mesh axis runs over, the one named last changes fastest.
Arguments:
- pair_rep: bfloat16 [384, 384, 256], P('row', 'col'), may hold values from -6 to 6
- single_rep: bfloat16 [384, 768], replicated, may hold values from -6 to 6
- length: int32 [1], replicated, may hold values from 192 to 384
- pair_gain: float32 [256], replicated, may hold values from 0.25 to 1.75
- pair_proj: bfloat16 [4, 256, 256], replicated, may hold values from -0.375 to 0.375
- bias_weight: bfloat16 [256, 8], replicated, may hold values from -12 to 12
- pair_out_weight: bfloat16 [256, 256], replicated, may hold values from -1 to 1
- single_gain: float32 [768], replicated, may hold values from 0.25 to 1.75
- single_proj: bfloat16 [4, 768, 768], P(None, None, 'col'), may hold values from -0.21875 to 0.21875
- bias_norm_gain: float32 [256], replicated, may hold values from 0.25 to 1.75
- single_bias_weight: bfloat16 [256, 16], replicated, may hold values from -12 to 12
- single_out_weight: bfloat16 [768, 768], P('col'), may hold values from -0.625 to 0.625
Outputs:
- pair_out: bfloat16 [384, 384, 256], P('row', 'col')
- single_out: bfloat16 [384, 768], P('row', 'col')
Inputs may be any that keep to these rules, and one draw needn't show every extreme that they name: Positions from length[0] on are padding and never serve as keys.
All inputs are finite; a program needn't handle non-finite values.
Results may differ from a plain program's by a relative error of at most 0.019.
Values may be sent and summed in bfloat16 or wider, within the bound.
A program may use at most 128 MiB of HBM per device.

v0:
```python
import math

import jax
import jax.numpy as jnp
from jax import lax
from jax.experimental import pallas as pl
from jax.experimental.pallas import tpu as pltpu
from jax.sharding import PartitionSpec as P

PAIR_HEADS = 8
PAIR_HEAD_DIM = 32
SINGLE_HEAD_DIM = 48
LOG2E = math.log2(math.e)

masked_value = -1e30
NT = (((1,), (1,)), ((), ()))


def normalize(values, scales):
    floated = values.astype(jnp.float32)
    center = jnp.mean(floated, axis=-1, keepdims=True)
    spread = jnp.mean(jnp.square(floated - center), axis=-1, keepdims=True)
    return ((floated - center) * lax.rsqrt(spread + 1e-05) * scales).astype(jnp.bfloat16)


def project(inputs, matrix):
    return jnp.dot(inputs, matrix, preferred_element_type=jnp.float32).astype(jnp.bfloat16)


def project_t(inputs, matrix):
    return lax.dot_general(inputs, matrix, NT, preferred_element_type=jnp.float32).astype(
        jnp.bfloat16
    )


def row_update(rep, gain, proj_ref, out_weight, bias_of):
    channels = rep.shape[1]
    half = channels // 2
    heads_per_half = PAIR_HEADS // 2
    normed = normalize(rep, gain)
    f32 = jnp.float32
    query = jnp.dot(normed, proj_ref[0], preferred_element_type=f32)
    query = (query * (LOG2E / math.sqrt(PAIR_HEAD_DIM))).astype(jnp.bfloat16)
    key = project(normed, proj_ref[1])
    value = project(normed, proj_ref[2])
    gate = jax.nn.sigmoid(jnp.dot(normed, proj_ref[3], preferred_element_type=f32))
    head_of_lane = lax.broadcasted_iota(jnp.int32, (1, half), 1) // PAIR_HEAD_DIM
    halves = []
    for side in range(2):
        span = slice(side * half, (side + 1) * half)
        q_half, k_half, v_half = query[:, span], key[:, span], value[:, span]
        top = bottom = None
        for sub in range(heads_per_half):
            head = side * heads_per_half + sub
            mine = head_of_lane == sub
            q_head = jnp.where(mine, q_half, jnp.zeros_like(q_half))
            scores = lax.dot_general(q_head, k_half, NT, preferred_element_type=f32)
            scores = scores + bias_of(head)
            peak = jnp.max(scores, axis=-1, keepdims=True)
            exponent = jnp.exp2(scores - peak).astype(jnp.bfloat16)
            v_ext = jnp.concatenate([v_half, jnp.ones_like(v_half)], axis=1)
            both = jnp.dot(exponent, v_ext, preferred_element_type=f32)
            num, den = both[:, :half], both[:, half:]
            top = num if top is None else jnp.where(mine, num, top)
            bottom = den if bottom is None else jnp.where(mine, den, bottom)
        halves.append(top / bottom)
    attended = jnp.concatenate(halves, axis=1)
    hidden = (gate * attended).astype(jnp.bfloat16)
    return (
        rep.astype(f32) + jnp.dot(hidden, out_weight, preferred_element_type=f32)
    ).astype(jnp.bfloat16)


def slot(ref, *index):
    return ref.at[index]


def window_kernel(
    length_ref, pair_ref, single_hbm, proj_hbm, out_weight_hbm, single_proj_hbm, single_out_hbm,
    gain_ref, tri_weight_ref, bias_gain_ref, head_weight_ref, single_gain_ref,
    pair_out_ref, single_new_ref,
    local, tri_kept, tri_ref, single_ref, proj_ref, out_weight_ref, single_proj_ref, single_out_ref,
    rest_ref, local_sem, weight_sem,
    slab, fresh, bands, bias_held, head_kept, head_sent, head_got, head_full,
    s_query, s_key, s_value, s_gate, part_sent, part_got,
    in_send, in_recv, in_own, out_send, out_recv, out_own,
    col_send, col_recv, col_own, chip_send, chip_recv, core_send, core_recv,
    head_send, head_recv, part_send, part_recv,
):
    f32 = jnp.float32
    slab_rows, cols, cols_here, channels = slab.shape
    rows, _, heads, rows_here, _ = bands.shape
    tokens = cols * cols_here
    chips = rows // 2
    row, col = lax.axis_index("row"), lax.axis_index("col")
    chip, core = row // 2, lax.rem(row, 2)
    partner = chip * 2 + 1 - core
    mesh_id = pl.DeviceIdType.MESH

    def peer(step):
        return lax.rem(col + step, cols)

    def chip_row(step):
        return lax.rem(chip + step, chips) * 2 + core

    def chip_back(step):
        return lax.rem(chip + chips - step, chips) * 2 + core

    def local_copy(part):
        span = pl.ds(part * slab_rows, slab_rows)
        return pltpu.make_async_copy(pair_ref.at[span], local.at[span], local_sem.at[part])

    weight_copies = [
        pltpu.make_async_copy(src, dst, weight_sem.at[i])
        for i, (src, dst) in enumerate(
            (
                (single_hbm, single_ref),
                (single_proj_hbm, single_proj_ref),
                (proj_hbm, proj_ref),
                (out_weight_hbm, out_weight_ref),
                (single_out_hbm, single_out_ref),
            )
        )
    ]
    for part in range(cols):
        local_copy(part).start()
    for copy in weight_copies:
        copy.start()

    barrier = pltpu.get_barrier_semaphore()
    for step in range(1, cols):
        pl.semaphore_signal(barrier, inc=1, device_id=(row, peer(step)), device_id_type=mesh_id)
    for step in range(1, chips):
        pl.semaphore_signal(barrier, inc=1, device_id=(chip_row(step), col), device_id_type=mesh_id)
    pl.semaphore_signal(barrier, inc=1, device_id=(partner, col), device_id_type=mesh_id)
    pl.semaphore_wait(barrier, cols + chips - 1)

    def remote(src, dst, send, recv, to):
        return pltpu.make_async_remote_copy(
            src_ref=src, dst_ref=dst, send_sem=send, recv_sem=recv,
            device_id=to, device_id_type=mesh_id,
        )

    near = cols // 2
    mirror = peer(near)

    def near_peer(step):
        return col // near * near + lax.rem(lax.rem(col, near) + step, near)

    own_steps = range(1, near)
    mirror_steps = range(near + 1, 2 * near)

    def col_copy(step):
        to = mirror if step == 0 else near_peer(step % near)
        src, place = (tri_ref, col) if step < near else (slot(bands, row, mirror), mirror)
        return remote(
            src, slot(bands, row, place), col_send.at[step], col_recv.at[step], (row, to)
        )

    def chip_copy(step):
        return remote(
            slot(bands, row), slot(bands, row), chip_send.at[step], chip_recv.at[step],
            (chip_row(step), col),
        )

    def core_copy(step):
        band = chip_back(step)
        return remote(
            slot(bands, band), slot(bands, band), core_send.at[step], core_recv.at[step],
            (partner, col),
        )

    def in_copy(s, step):
        to = peer(step)
        return remote(
            slot(pair_ref, to * slab_rows + s), slot(slab, s, col),
            in_send.at[s, step], in_recv.at[s, step], (row, to),
        )

    def own_in(s):
        return pltpu.make_async_copy(
            slot(pair_ref, col * slab_rows + s), slot(slab, s, col), in_own.at[s]
        )

    def out_copy(s, step):
        to = peer(step)
        return remote(
            slot(fresh, s, to), slot(pair_out_ref, col * slab_rows + s),
            out_send.at[s, step], out_recv.at[s, step], (row, to),
        )

    def own_out(s):
        return pltpu.make_async_copy(
            slot(fresh, s, col), slot(pair_out_ref, col * slab_rows + s), out_own.at[s]
        )

    def head_copy(step):
        to = peer(step)
        return remote(
            slot(head_sent, to), slot(head_got, col), head_send.at[step], head_recv.at[step],
            (row, to),
        )

    def part_copy(step):
        to = peer(step)
        return remote(
            slot(part_sent, to), slot(part_got, step), part_send.at[step], part_recv.at[step],
            (row, to),
        )

    def bring_row(s):
        own_in(s).start()
        for step in range(1, cols):
            in_copy(s, step).start()

    bring_row(0)
    group = math.gcd(slab_rows, 6)
    for part in range(cols):
        local_copy(part).wait()

        @pl.loop(0, slab_rows // group)
        def _(i):
            for j in range(group):
                r = part * slab_rows + i * group + j
                tri_kept[:, r, :] = lax.dot_general(
                    tri_weight_ref[...], normalize(local[r], gain_ref[...]), NT,
                    preferred_element_type=f32,
                )

    tri_ref[...] = tri_kept[...].astype(jnp.bfloat16)
    for step in (0, *own_steps):
        col_copy(step).start()
    own_block = pltpu.make_async_copy(tri_ref, slot(bands, row, col), col_own)
    own_block.start()

    ahead = min(3, slab_rows)
    for s in range(1, ahead):
        bring_row(s)
    col_copy(0).wait_recv()
    for step in mirror_steps:
        col_copy(step).start()

    @pl.loop(ahead, slab_rows)
    def _(s):
        bring_row(s)

    for copy in weight_copies:
        copy.wait()

    for step in (*own_steps, *mirror_steps):
        col_copy(step).wait_recv()
    own_block.wait()
    for step in range(1, chips):
        chip_copy(step).start()
    core_copy(0).start()

    s_normed = normalize(single_ref[...], single_gain_ref[...])
    s_key[...] = project_t(s_normed, single_proj_ref[1])
    s_value[...] = project_t(s_normed, single_proj_ref[2])
    width = s_key.shape[1]
    my_rows = pl.ds(pl.multiple_of(row * rows_here, rows_here), rows_here)
    for part in range(cols):

        @pl.when(col == part)
        def _():
            rest_ref[...] = single_ref[my_rows, part * width : (part + 1) * width]

    mine = normalize(
        single_ref[my_rows, :],
        single_gain_ref[...],
    )
    s_query[...] = (
        lax.dot_general(mine, single_proj_ref[0], NT, preferred_element_type=f32)
        * (LOG2E / math.sqrt(SINGLE_HEAD_DIM))
    ).astype(jnp.bfloat16)
    s_gate[...] = jax.nn.sigmoid(
        lax.dot_general(mine, single_proj_ref[3], NT, preferred_element_type=f32)
    )

    def take_band(band):
        start = pl.multiple_of(band * rows_here, rows_here)
        for part in range(cols):
            usable = (
                lax.broadcasted_iota(jnp.int32, (1, 1, cols_here), 2) + part * cols_here
                < length_ref[0]
            )
            piece = bands[band, part].astype(f32) * LOG2E
            bias_held[:, pl.ds(start, rows_here), part * cols_here : (part + 1) * cols_here] = (
                jnp.where(usable, piece, masked_value)
            )

    take_band(row)
    for step in range(1, chips):
        chip_copy(step).wait_recv()
        core_copy(step).start()
        take_band(chip_back(step))
    for step in range(chips):
        core_copy(step).wait_recv()
        take_band(chip_back(step) + 1 - 2 * core)

    early = 2 * slab_rows // 3
    late = slab_rows - slab_rows // 6

    def one_row(s):
        own_in(s).wait()
        for step in range(1, cols):
            in_copy(s, step).wait_recv()
        rep = slab[s].reshape(tokens, channels)
        updated = row_update(
            rep, gain_ref[...], proj_ref, out_weight_ref[...], lambda head: bias_held[head]
        )
        fresh[s] = updated.reshape(cols, cols_here, channels)
        again = normalize(updated, bias_gain_ref[...])
        head_kept[:, s, :] = lax.dot_general(
            head_weight_ref[...], again, NT, preferred_element_type=f32
        )

    def send_row(s):
        own_out(s).start()
        for step in range(1, cols):
            out_copy(s, step).start()

    @pl.loop(0, slab_rows)
    def _(s):
        one_row(s)

        @pl.when(s < early)
        def _():
            send_row(s)

    head_sent[...] = head_kept[...].astype(jnp.bfloat16).reshape(head_sent.shape)
    for step in range(1, cols):
        head_copy(step).start()

    @pl.loop(early, late)
    def _(s):
        send_row(s)

    for step in range(1, cols):
        head_copy(step).wait_recv()
    for part in range(cols):
        span = slice(part * slab_rows, (part + 1) * slab_rows)

        @pl.when(col == part)
        def _():
            head_full[:, span, :] = head_sent[part].astype(f32) * LOG2E

        @pl.when(col != part)
        def _():
            head_full[:, span, :] = head_got[part].astype(f32) * LOG2E

    s_heads = head_full.shape[0]
    usable = lax.broadcasted_iota(jnp.int32, (1, tokens), 1) < length_ref[0]
    head_of_lane = lax.broadcasted_iota(jnp.int32, (1, width), 1) // SINGLE_HEAD_DIM
    blended = jnp.zeros((rows_here, width), f32)
    for head in range(s_heads):
        here = head_of_lane == head
        q_head = jnp.where(here, s_query[...], jnp.zeros_like(s_query[...]))
        scores = lax.dot_general(q_head, s_key[...], NT, preferred_element_type=f32)
        scores = jnp.where(usable, scores + head_full[head], masked_value)
        exponent = jnp.exp2(scores - jnp.max(scores, axis=-1, keepdims=True))
        total = jnp.sum(exponent, axis=-1, keepdims=True)
        weights = (exponent / total).astype(jnp.bfloat16)
        blended = jnp.where(
            here, jnp.dot(weights, s_value[...], preferred_element_type=f32), blended
        )
    s_hidden = (s_gate[...] * blended).astype(jnp.bfloat16)
    share = jnp.dot(s_hidden, single_out_ref[...], preferred_element_type=f32)
    for part in range(cols):
        part_sent[part] = share[:, part * width : (part + 1) * width].astype(jnp.bfloat16)
    for step in range(1, cols):
        part_copy(step).start()

    @pl.loop(late, slab_rows)
    def _(s):
        send_row(s)

    total = rest_ref[...].astype(f32) + part_sent[col].astype(f32)
    for step in range(1, cols):
        part_copy(step).wait_recv()
        total = total + part_got[step].astype(f32)
    single_new_ref[...] = total.astype(jnp.bfloat16)

    for step in range(1, cols):
        head_copy(step).wait_send()
        part_copy(step).wait_send()
    for step in (0, *own_steps, *mirror_steps):
        col_copy(step).wait_send()
    for step in range(1, chips):
        chip_copy(step).wait_send()
    for step in range(chips):
        core_copy(step).wait_send()

    @pl.loop(0, slab_rows)
    def _(s):
        own_out(s).wait()
        for step in range(1, cols):
            in_copy(s, step).wait_send()
            out_copy(s, step).wait_send()
            out_copy(s, step).wait_recv()


def per_device(
    pair_rep,
    single_rep,
    length,
    pair_gain,
    pair_proj,
    bias_weight,
    pair_out_weight,
    single_gain,
    single_proj,
    bias_norm_gain,
    single_bias_weight,
    single_out_weight,
):
    rows_here, cols_here, channels = pair_rep.shape
    rows, cols = lax.axis_size("row"), lax.axis_size("col")
    tokens = rows_here * rows
    slab_rows = rows_here // cols
    chips = rows // 2
    heads = bias_weight.shape[1]
    single_heads = single_bias_weight.shape[1]
    heads_here = single_heads // cols
    width = single_proj.shape[2]
    single_proj_t = single_proj.transpose(0, 2, 1)
    bf16, f32 = jnp.bfloat16, jnp.float32
    dma = pltpu.SemaphoreType.DMA
    anywhere = pl.BlockSpec(memory_space=pl.ANY)
    held = pl.BlockSpec(memory_space=pltpu.VMEM)
    pair_out, single_out = pl.pallas_call(
        window_kernel,
        in_specs=[pl.BlockSpec(memory_space=pltpu.SMEM)] + [anywhere] * 6 + [held] * 5,
        out_specs=[anywhere, held],
        out_shape=[
            jax.ShapeDtypeStruct(pair_rep.shape, bf16),
            jax.ShapeDtypeStruct((rows_here, width), bf16),
        ],
        scratch_shapes=[
            pltpu.VMEM(pair_rep.shape, bf16),
            pltpu.VMEM((heads, rows_here, cols_here), f32),
            pltpu.VMEM((heads, rows_here, cols_here), bf16),
            pltpu.VMEM(single_rep.shape, bf16),
            pltpu.VMEM(pair_proj.shape, bf16),
            pltpu.VMEM(pair_out_weight.shape, bf16),
            pltpu.VMEM(single_proj_t.shape, bf16),
            pltpu.VMEM(single_out_weight.shape, bf16),
            pltpu.VMEM((rows_here, width), bf16),
            dma((cols,)),
            dma((5,)),
            pltpu.VMEM((slab_rows, cols, cols_here, channels), bf16),
            pltpu.VMEM((slab_rows, cols, cols_here, channels), bf16),
            pltpu.VMEM((rows, cols, heads, rows_here, cols_here), bf16),
            pltpu.VMEM((heads, tokens, tokens), f32),
            pltpu.VMEM((single_heads, slab_rows, tokens), f32),
            pltpu.VMEM((cols, heads_here, slab_rows, tokens), bf16),
            pltpu.VMEM((cols, heads_here, slab_rows, tokens), bf16),
            pltpu.VMEM((heads_here, rows_here, tokens), f32),
            pltpu.VMEM((rows_here, width), bf16),
            pltpu.VMEM((tokens, width), bf16),
            pltpu.VMEM((tokens, width), bf16),
            pltpu.VMEM((rows_here, width), f32),
            pltpu.VMEM((cols, rows_here, width), bf16),
            pltpu.VMEM((cols, rows_here, width), bf16),
            dma((slab_rows, cols)),
            dma((slab_rows, cols)),
            dma((slab_rows,)),
            dma((slab_rows, cols)),
            dma((slab_rows, cols)),
            dma((slab_rows,)),
            dma((cols,)),
            dma((cols,)),
            dma,
            dma((chips,)),
            dma((chips,)),
            dma((chips,)),
            dma((chips,)),
            dma((cols,)),
            dma((cols,)),
            dma((cols,)),
            dma((cols,)),
        ],
        compiler_params=pltpu.CompilerParams(
            collective_id=0, has_side_effects=True, vmem_limit_bytes=60 * 2**20
        ),
        name="window",
    )(
        length, pair_rep, single_rep, pair_proj, pair_out_weight, single_proj_t, single_out_weight,
        pair_gain, bias_weight.T, bias_norm_gain, single_bias_weight.T, single_gain,
    )
    return (pair_out, single_out)


def solution(mesh):
    in_specs = (
        P("row", "col", None),
        P(),
        P(),
        P(),
        P(),
        P(),
        P(),
        P(),
        P(None, None, "col"),
        P(),
        P(),
        P("col", None),
    )
    out_specs = (P("row", "col", None), P("row", "col"))
    return jax.shard_map(
        per_device, mesh=mesh, in_specs=in_specs, out_specs=out_specs, check_vma=False
    )
```

profile of v0, /device:TPU:0, one launch (start us, length us, event | category | flops | bytes accessed | tf_op | source)
XLA Modules:
  0.0 127.3 jit_solution(8531980896876777988)
XLA Ops:
  1.3 122.2 %window.1 = (bf16[48,96,256]{2,1,0:T(8,128)(2,1)}, bf16[48,192]{1,0:T(8,128)(2,1)}) custom-call(s32[1]{0:T(128)S(6)} %copy.16.length_ref, bf16[48,96,256]{2,1,0:T(8,128)(2,1)} %pair_ref.1, bf16[384,768]{1,0:T(8,128)(2,1)} %single_hbm.1, bf16[4,256,256]{2,1,0:T(8,128)(2,1)} %proj_hbm.1, bf16[256,256]{1,0:T(8,128)(2,1)} %out_weight_hbm.1, ...), custom_call_target="tpu_custom_call" | custom-call | tf_op jit(solution)/shard_map/window/pallas_call | solution.py:431
  123.4 0.0 copy-start
  123.5 3.2 %copy.17 = bf16[48,96,256]{2,1,0:T(8,128)(2,1)} copy(bf16[48,96,256]{2,1,0:T(8,128)(2,1)} %get-tuple-element.4) | data formatting | bytes 4718592
  126.7 0.0 copy-done
  126.7 0.6 copy.18
Async XLA Ops:
  123.4 3.2 %copy-start = (bf16[48,192]{1,0:T(8,128)(2,1)S(1)}, bf16[48,192]{1,0:T(8,128)(2,1)}, u32[]{:S(2)}) copy-start(bf16[48,192]{1,0:T(8,128)(2,1)} %get-tuple-element.5) | copy-start | bytes 55300
where the time goes:
time: 127 us
  Pallas kernels  122 us (96%)
  local copies, waits for them, and re-layouts  3.84 us (3%)
  between operations  1.3 us (1%)
    pallas_call x1, Pallas kernels, per_device(): pl.pallas_call(window_kernel, in_specs=[pl.BlockSpec(memory_space=pltpu.S...  122 us
    unnamed x4, local copies, waits for them, and re-layouts  3.84 us

commit v1 on v0

--- a/solution.py
+++ b/solution.py
@@ -76,15 +76,16 @@
 
 
 def window_kernel(
-    length_ref, pair_ref, single_hbm, proj_hbm, out_weight_hbm, single_proj_hbm, single_out_hbm,
-    gain_ref, tri_weight_ref, bias_gain_ref, head_weight_ref, single_gain_ref,
+    length_hbm, pair_ref, single_hbm, proj_hbm, out_weight_hbm, single_proj_hbm, single_out_hbm,
+    gain_hbm, tri_weight_hbm, bias_gain_hbm, head_weight_hbm, single_gain_hbm,
     pair_out_ref, single_new_ref,
     local, tri_kept, tri_ref, single_ref, proj_ref, out_weight_ref, single_proj_ref, single_out_ref,
+    gain_ref, tri_weight_ref, bias_gain_ref, head_weight_ref, single_gain_ref, length_ref,
     rest_ref, local_sem, weight_sem,
     slab, fresh, bands, bias_held, head_kept, head_sent, head_got, head_full,
     s_query, s_key, s_value, s_gate, part_sent, part_got,
-    in_send, in_recv, in_own, out_send, out_recv, out_own,
-    col_send, col_recv, col_own, chip_send, chip_recv, core_send, core_recv,
+    in_send, in_recv, out_send, out_recv,
+    col_send, col_recv, chip_send, chip_recv, core_send, core_recv,
     head_send, head_recv, part_send, part_recv,
 ):
     f32 = jnp.float32
@@ -114,6 +115,12 @@
         pltpu.make_async_copy(src, dst, weight_sem.at[i])
         for i, (src, dst) in enumerate(
             (
+                (gain_hbm, gain_ref),
+                (tri_weight_hbm, tri_weight_ref),
+                (length_hbm, length_ref),
+                (bias_gain_hbm, bias_gain_ref),
+                (head_weight_hbm, head_weight_ref),
+                (single_gain_hbm, single_gain_ref),
                 (single_hbm, single_ref),
                 (single_proj_hbm, single_proj_ref),
                 (proj_hbm, proj_ref),
@@ -122,18 +129,20 @@
             )
         )
     ]
-    for part in range(cols):
-        local_copy(part).start()
-    for copy in weight_copies:
-        copy.start()
-
     barrier = pltpu.get_barrier_semaphore()
     for step in range(1, cols):
         pl.semaphore_signal(barrier, inc=1, device_id=(row, peer(step)), device_id_type=mesh_id)
     for step in range(1, chips):
         pl.semaphore_signal(barrier, inc=1, device_id=(chip_row(step), col), device_id_type=mesh_id)
     pl.semaphore_signal(barrier, inc=1, device_id=(partner, col), device_id_type=mesh_id)
-    pl.semaphore_wait(barrier, cols + chips - 1)
+    for copy in weight_copies[:2]:
+        copy.start()
+    for part in range(cols):
+        local_copy(part).start()
+    for copy in weight_copies[2:]:
+        copy.start()
+    with jax.named_scope('bar'):
+        pl.semaphore_wait(barrier, cols + chips - 1)
 
     def remote(src, dst, send, recv, to):
         return pltpu.make_async_remote_copy(
@@ -154,19 +163,19 @@
         to = mirror if step == 0 else near_peer(step % near)
         src, place = (tri_ref, col) if step < near else (slot(bands, row, mirror), mirror)
         return remote(
-            src, slot(bands, row, place), col_send.at[step], col_recv.at[step], (row, to)
+            src, slot(bands, row, place), col_send, col_recv.at[min(step, 1)], (row, to)
         )
 
     def chip_copy(step):
         return remote(
-            slot(bands, row), slot(bands, row), chip_send.at[step], chip_recv.at[step],
+            slot(bands, row), slot(bands, row), chip_send, chip_recv.at[step - 1],
             (chip_row(step), col),
         )
 
     def core_copy(step):
         band = chip_back(step)
         return remote(
-            slot(bands, band), slot(bands, band), core_send.at[step], core_recv.at[step],
+            slot(bands, band), slot(bands, band), core_send, core_recv.at[step],
             (partner, col),
         )
 
@@ -174,39 +183,44 @@
         to = peer(step)
         return remote(
             slot(pair_ref, to * slab_rows + s), slot(slab, s, col),
-            in_send.at[s, step], in_recv.at[s, step], (row, to),
+            in_send, in_recv.at[s], (row, to),
         )
 
     def own_in(s):
         return pltpu.make_async_copy(
-            slot(pair_ref, col * slab_rows + s), slot(slab, s, col), in_own.at[s]
+            slot(pair_ref, col * slab_rows + s), slot(slab, s, col), in_recv.at[s]
         )
 
     def out_copy(s, step):
         to = peer(step)
         return remote(
             slot(fresh, s, to), slot(pair_out_ref, col * slab_rows + s),
-            out_send.at[s, step], out_recv.at[s, step], (row, to),
+            out_send, out_recv, (row, to),
         )
 
     def own_out(s):
         return pltpu.make_async_copy(
-            slot(fresh, s, col), slot(pair_out_ref, col * slab_rows + s), out_own.at[s]
+            slot(fresh, s, col), slot(pair_out_ref, col * slab_rows + s), out_recv
         )
 
     def head_copy(step):
         to = peer(step)
         return remote(
-            slot(head_sent, to), slot(head_got, col), head_send.at[step], head_recv.at[step],
+            slot(head_sent, to), slot(head_got, col), head_send, head_recv,
             (row, to),
         )
 
     def part_copy(step):
         to = peer(step)
         return remote(
-            slot(part_sent, to), slot(part_got, step), part_send.at[step], part_recv.at[step],
+            slot(part_sent, to), slot(part_got, step), part_send, part_recv,
             (row, to),
         )
+
+    def settle(ref, sem):
+        pltpu.make_async_copy(ref, ref, sem).wait()
+
+    others = pl.ds(0, cols - 1)
 
     def bring_row(s):
         own_in(s).start()
@@ -214,29 +228,33 @@
             in_copy(s, step).start()
 
     bring_row(0)
-    group = math.gcd(slab_rows, 6)
-    for part in range(cols):
-        local_copy(part).wait()
-
-        @pl.loop(0, slab_rows // group)
-        def _(i):
-            for j in range(group):
-                r = part * slab_rows + i * group + j
-                tri_kept[:, r, :] = lax.dot_general(
-                    tri_weight_ref[...], normalize(local[r], gain_ref[...]), NT,
-                    preferred_element_type=f32,
-                )
+    for copy in weight_copies[:2]:
+        copy.wait()
+    with jax.named_scope('tri'):
+        group = math.gcd(slab_rows, 6)
+        for part in range(cols):
+            local_copy(part).wait()
+
+            @pl.loop(0, slab_rows // group)
+            def _(i):
+                for j in range(group):
+                    r = part * slab_rows + i * group + j
+                    tri_kept[:, r, :] = lax.dot_general(
+                        tri_weight_ref[...], normalize(local[r], gain_ref[...]), NT,
+                        preferred_element_type=f32,
+                    )
 
     tri_ref[...] = tri_kept[...].astype(jnp.bfloat16)
     for step in (0, *own_steps):
         col_copy(step).start()
-    own_block = pltpu.make_async_copy(tri_ref, slot(bands, row, col), col_own)
+    own_block = pltpu.make_async_copy(tri_ref, slot(bands, row, col), col_recv.at[1])
     own_block.start()
 
     ahead = min(3, slab_rows)
     for s in range(1, ahead):
         bring_row(s)
-    col_copy(0).wait_recv()
+    with jax.named_scope('waitmirror'):
+        col_copy(0).wait_recv()
     for step in mirror_steps:
         col_copy(step).start()
 
@@ -244,38 +262,38 @@
     def _(s):
         bring_row(s)
 
-    for copy in weight_copies:
+    for copy in weight_copies[2:]:
         copy.wait()
 
-    for step in (*own_steps, *mirror_steps):
-        col_copy(step).wait_recv()
-    own_block.wait()
+    with jax.named_scope('waitcols'):
+        settle(slot(bands, row, others), col_recv.at[1])
     for step in range(1, chips):
         chip_copy(step).start()
     core_copy(0).start()
 
-    s_normed = normalize(single_ref[...], single_gain_ref[...])
-    s_key[...] = project_t(s_normed, single_proj_ref[1])
-    s_value[...] = project_t(s_normed, single_proj_ref[2])
-    width = s_key.shape[1]
-    my_rows = pl.ds(pl.multiple_of(row * rows_here, rows_here), rows_here)
-    for part in range(cols):
-
-        @pl.when(col == part)
-        def _():
-            rest_ref[...] = single_ref[my_rows, part * width : (part + 1) * width]
-
-    mine = normalize(
-        single_ref[my_rows, :],
-        single_gain_ref[...],
-    )
-    s_query[...] = (
-        lax.dot_general(mine, single_proj_ref[0], NT, preferred_element_type=f32)
-        * (LOG2E / math.sqrt(SINGLE_HEAD_DIM))
-    ).astype(jnp.bfloat16)
-    s_gate[...] = jax.nn.sigmoid(
-        lax.dot_general(mine, single_proj_ref[3], NT, preferred_element_type=f32)
-    )
+    with jax.named_scope('sproj'):
+        s_normed = normalize(single_ref[...], single_gain_ref[...])
+        s_key[...] = project_t(s_normed, single_proj_ref[1])
+        s_value[...] = project_t(s_normed, single_proj_ref[2])
+        width = s_key.shape[1]
+        my_rows = pl.ds(pl.multiple_of(row * rows_here, rows_here), rows_here)
+        for part in range(cols):
+
+            @pl.when(col == part)
+            def _():
+                rest_ref[...] = single_ref[my_rows, part * width : (part + 1) * width]
+
+        mine = normalize(
+            single_ref[my_rows, :],
+            single_gain_ref[...],
+        )
+        s_query[...] = (
+            lax.dot_general(mine, single_proj_ref[0], NT, preferred_element_type=f32)
+            * (LOG2E / math.sqrt(SINGLE_HEAD_DIM))
+        ).astype(jnp.bfloat16)
+        s_gate[...] = jax.nn.sigmoid(
+            lax.dot_general(mine, single_proj_ref[3], NT, preferred_element_type=f32)
+        )
 
     def take_band(band):
         start = pl.multiple_of(band * rows_here, rows_here)
@@ -289,22 +307,21 @@
                 jnp.where(usable, piece, masked_value)
             )
 
-    take_band(row)
-    for step in range(1, chips):
-        chip_copy(step).wait_recv()
-        core_copy(step).start()
-        take_band(chip_back(step))
-    for step in range(chips):
-        core_copy(step).wait_recv()
-        take_band(chip_back(step) + 1 - 2 * core)
+    with jax.named_scope('bands'):
+        take_band(row)
+        for step in range(1, chips):
+            chip_copy(step).wait_recv()
+            core_copy(step).start()
+            take_band(chip_back(step))
+        for step in range(chips):
+            core_copy(step).wait_recv()
+            take_band(chip_back(step) + 1 - 2 * core)
 
     early = 2 * slab_rows // 3
     late = slab_rows - slab_rows // 6
 
     def one_row(s):
-        own_in(s).wait()
-        for step in range(1, cols):
-            in_copy(s, step).wait_recv()
+        settle(slot(slab, s), in_recv.at[s])
         rep = slab[s].reshape(tokens, channels)
         updated = row_update(
             rep, gain_ref[...], proj_ref, out_weight_ref[...], lambda head: bias_held[head]
@@ -320,13 +337,14 @@
         for step in range(1, cols):
             out_copy(s, step).start()
 
-    @pl.loop(0, slab_rows)
-    def _(s):
-        one_row(s)
-
-        @pl.when(s < early)
-        def _():
-            send_row(s)
+    with jax.named_scope('rows'):
+        @pl.loop(0, slab_rows)
+        def _(s):
+            one_row(s)
+
+            @pl.when(s < early)
+            def _():
+                send_row(s)
 
     head_sent[...] = head_kept[...].astype(jnp.bfloat16).reshape(head_sent.shape)
     for step in range(1, cols):
@@ -336,8 +354,8 @@
     def _(s):
         send_row(s)
 
-    for step in range(1, cols):
-        head_copy(step).wait_recv()
+    with jax.named_scope('headwait'):
+        settle(slot(head_got, others), head_recv)
     for part in range(cols):
         span = slice(part * slab_rows, (part + 1) * slab_rows)
 
@@ -349,55 +367,50 @@
         def _():
             head_full[:, span, :] = head_got[part].astype(f32) * LOG2E
 
-    s_heads = head_full.shape[0]
-    usable = lax.broadcasted_iota(jnp.int32, (1, tokens), 1) < length_ref[0]
-    head_of_lane = lax.broadcasted_iota(jnp.int32, (1, width), 1) // SINGLE_HEAD_DIM
-    blended = jnp.zeros((rows_here, width), f32)
-    for head in range(s_heads):
-        here = head_of_lane == head
-        q_head = jnp.where(here, s_query[...], jnp.zeros_like(s_query[...]))
-        scores = lax.dot_general(q_head, s_key[...], NT, preferred_element_type=f32)
-        scores = jnp.where(usable, scores + head_full[head], masked_value)
-        exponent = jnp.exp2(scores - jnp.max(scores, axis=-1, keepdims=True))
-        total = jnp.sum(exponent, axis=-1, keepdims=True)
-        weights = (exponent / total).astype(jnp.bfloat16)
-        blended = jnp.where(
-            here, jnp.dot(weights, s_value[...], preferred_element_type=f32), blended
-        )
-    s_hidden = (s_gate[...] * blended).astype(jnp.bfloat16)
-    share = jnp.dot(s_hidden, single_out_ref[...], preferred_element_type=f32)
-    for part in range(cols):
-        part_sent[part] = share[:, part * width : (part + 1) * width].astype(jnp.bfloat16)
-    for step in range(1, cols):
-        part_copy(step).start()
+    with jax.named_scope('sattn'):
+        s_heads = head_full.shape[0]
+        usable = lax.broadcasted_iota(jnp.int32, (1, tokens), 1) < length_ref[0]
+        head_of_lane = lax.broadcasted_iota(jnp.int32, (1, width), 1) // SINGLE_HEAD_DIM
+        blended = jnp.zeros((rows_here, width), f32)
+        for head in range(s_heads):
+            here = head_of_lane == head
+            q_head = jnp.where(here, s_query[...], jnp.zeros_like(s_query[...]))
+            scores = lax.dot_general(q_head, s_key[...], NT, preferred_element_type=f32)
+            scores = jnp.where(usable, scores + head_full[head], masked_value)
+            exponent = jnp.exp2(scores - jnp.max(scores, axis=-1, keepdims=True))
+            total = jnp.sum(exponent, axis=-1, keepdims=True)
+            weights = (exponent / total).astype(jnp.bfloat16)
+            blended = jnp.where(
+                here, jnp.dot(weights, s_value[...], preferred_element_type=f32), blended
+            )
+        s_hidden = (s_gate[...] * blended).astype(jnp.bfloat16)
+        share = jnp.dot(s_hidden, single_out_ref[...], preferred_element_type=f32)
+        for part in range(cols):
+            part_sent[part] = share[:, part * width : (part + 1) * width].astype(jnp.bfloat16)
+        for step in range(1, cols):
+            part_copy(step).start()
 
     @pl.loop(late, slab_rows)
     def _(s):
         send_row(s)
 
-    total = rest_ref[...].astype(f32) + part_sent[col].astype(f32)
-    for step in range(1, cols):
-        part_copy(step).wait_recv()
-        total = total + part_got[step].astype(f32)
-    single_new_ref[...] = total.astype(jnp.bfloat16)
-
-    for step in range(1, cols):
-        head_copy(step).wait_send()
-        part_copy(step).wait_send()
-    for step in (0, *own_steps, *mirror_steps):
-        col_copy(step).wait_send()
-    for step in range(1, chips):
-        chip_copy(step).wait_send()
-    for step in range(chips):
-        core_copy(step).wait_send()
-
-    @pl.loop(0, slab_rows)
-    def _(s):
-        own_out(s).wait()
+    with jax.named_scope('part'):
+        total = rest_ref[...].astype(f32) + part_sent[col].astype(f32)
+        settle(slot(part_got, others), part_recv)
         for step in range(1, cols):
-            in_copy(s, step).wait_send()
-            out_copy(s, step).wait_send()
-            out_copy(s, step).wait_recv()
+            total = total + part_got[step].astype(f32)
+        single_new_ref[...] = total.astype(jnp.bfloat16)
+
+    with jax.named_scope('drain'):
+        settle(slot(head_sent, others), head_send)
+        settle(slot(part_sent, others), part_send)
+        settle(slot(bands, row, others), col_send)
+        settle(slot(bands, pl.ds(0, chips - 1)), chip_send)
+        settle(slot(bands, pl.ds(0, chips)), core_send)
+        sent = slot(local, pl.ds(0, slab_rows * (cols - 1)))
+        settle(sent, in_send)
+        settle(sent, out_send)
+        settle(pair_out_ref, out_recv)
 
 
 def per_device(
@@ -427,14 +440,15 @@
     bf16, f32 = jnp.bfloat16, jnp.float32
     dma = pltpu.SemaphoreType.DMA
     anywhere = pl.BlockSpec(memory_space=pl.ANY)
+    stay = pl.BlockSpec(memory_space=pltpu.HBM)
     held = pl.BlockSpec(memory_space=pltpu.VMEM)
     pair_out, single_out = pl.pallas_call(
         window_kernel,
-        in_specs=[pl.BlockSpec(memory_space=pltpu.SMEM)] + [anywhere] * 6 + [held] * 5,
+        in_specs=[stay] * 12,
         out_specs=[anywhere, held],
         out_shape=[
-            jax.ShapeDtypeStruct(pair_rep.shape, bf16),
-            jax.ShapeDtypeStruct((rows_here, width), bf16),
+            pltpu.VMEM(pair_rep.shape, bf16),
+            pltpu.VMEM((rows_here, width), bf16),
         ],
         scratch_shapes=[
             pltpu.VMEM(pair_rep.shape, bf16),
@@ -445,9 +459,15 @@
             pltpu.VMEM(pair_out_weight.shape, bf16),
             pltpu.VMEM(single_proj_t.shape, bf16),
             pltpu.VMEM(single_out_weight.shape, bf16),
+            pltpu.VMEM(pair_gain.shape, f32),
+            pltpu.VMEM((heads, channels), bf16),
+            pltpu.VMEM(bias_norm_gain.shape, f32),
+            pltpu.VMEM((single_heads, channels), bf16),
+            pltpu.VMEM(single_gain.shape, f32),
+            pltpu.SMEM(length.shape, jnp.int32),
             pltpu.VMEM((rows_here, width), bf16),
             dma((cols,)),
-            dma((5,)),
+            dma((11,)),
             pltpu.VMEM((slab_rows, cols, cols_here, channels), bf16),
             pltpu.VMEM((slab_rows, cols, cols_here, channels), bf16),
             pltpu.VMEM((rows, cols, heads, rows_here, cols_here), bf16),
@@ -462,26 +482,23 @@
             pltpu.VMEM((rows_here, width), f32),
             pltpu.VMEM((cols, rows_here, width), bf16),
             pltpu.VMEM((cols, rows_here, width), bf16),
-            dma((slab_rows, cols)),
-            dma((slab_rows, cols)),
+            dma,
             dma((slab_rows,)),
-            dma((slab_rows, cols)),
-            dma((slab_rows, cols)),
-            dma((slab_rows,)),
-            dma((cols,)),
-            dma((cols,)),
+            dma,
+            dma,
+            dma,
+            dma((2,)),
+            dma,
+            dma((chips - 1,)),
             dma,
             dma((chips,)),
-            dma((chips,)),
-            dma((chips,)),
-            dma((chips,)),
-            dma((cols,)),
-            dma((cols,)),
-            dma((cols,)),
-            dma((cols,)),
+            dma,
+            dma,
+            dma,
+            dma,
         ],
         compiler_params=pltpu.CompilerParams(
-            collective_id=0, has_side_effects=True, vmem_limit_bytes=60 * 2**20
+            collective_id=0, has_side_effects=True, vmem_limit_bytes=56 * 2**20
         ),
         name="window",
     )(

time: 127 us -> 122 us (0.961)
  Pallas kernels: 122 us -> 119 us
  local copies, waits for them, and re-layouts: 3.84 us -> 2.02 us
    pallas_call x1, Pallas kernels: 122 us -> 119 us  [per_device(): pl.pallas_call(window_kernel, in_specs=[stay] * 12, out_specs=[anywhere,...]
    unnamed x4 -> x2, local copies, waits for them, and re-layouts: 3.84 us -> 2.02 us
where the time goes in v1:
time: 122 us
  Pallas kernels  119 us (98%)
  local copies, waits for them, and re-layouts  2.02 us (2%)
  between operations  1.29 us (1%)
    pallas_call x1, Pallas kernels, per_device(): pl.pallas_call(window_kernel, in_specs=[stay] * 12, out_specs=[anywhere,...  119 us

profile of v1, /device:TPU:0, one launch (start us, length us, event | category | flops | bytes accessed | tf_op | source)
XLA Modules:
  0.0 122.1 jit_solution(12181413789413552192)
XLA Ops:
  1.3 118.8 %window.1 = (bf16[48,96,256]{2,1,0:T(8,128)(2,1)S(1)}, bf16[48,192]{1,0:T(8,128)(2,1)S(1)}) custom-call(s32[1]{0:T(128)S(6)} %copy.18.length_hbm, bf16[48,96,256]{2,1,0:T(8,128)(2,1)} %pair_ref.1, bf16[384,768]{1,0:T(8,128)(2,1)} %single_hbm.1, bf16[4,256,256]{2,1,0:T(8,128)(2,1)} %proj_hbm.1, bf16[256,256]{1,0:T(8,128)(2,1)} %out_weight_hbm.1, ...), custom_call_target="tpu_custom_call" | custom-call | tf_op jit(solution)/shard_map/window/pallas_call | solution.py:445
  120.1 1.4 %copy.16 = bf16[48,96,256]{2,1,0:T(8,128)(2,1)} copy(bf16[48,96,256]{2,1,0:T(8,128)(2,1)S(1)} %get-tuple-element.2) | data formatting | bytes 4718592
  121.5 0.6 copy.17

commit v2 on v1

--- a/solution.py
+++ b/solution.py
@@ -83,10 +83,10 @@
     gain_ref, tri_weight_ref, bias_gain_ref, head_weight_ref, single_gain_ref, length_ref,
     rest_ref, local_sem, weight_sem,
     slab, fresh, bands, bias_held, head_kept, head_sent, head_got, head_full,
-    s_query, s_key, s_value, s_gate, part_sent, part_got,
+    s_query, s_key, s_value, s_gate, part_sent, part_got, merged_sent, merged_got,
     in_send, in_recv, out_send, out_recv,
     col_send, col_recv, chip_send, chip_recv, core_send, core_recv,
-    head_send, head_recv, part_send, part_recv,
+    head_send, head_recv, part_send, part_recv, merged_send, merged_recv,
 ):
     f32 = jnp.float32
     slab_rows, cols, cols_here, channels = slab.shape
@@ -210,12 +210,16 @@
             (row, to),
         )
 
+    lane, half = lax.rem(col, near), col // near
+
     def part_copy(step):
-        to = peer(step)
-        return remote(
-            slot(part_sent, to), slot(part_got, step), part_send, part_recv,
-            (row, to),
-        )
+        return remote(
+            slot(part_sent, lax.rem(lane + step, near)), slot(part_got, step),
+            part_send, part_recv, (row, near_peer(step)),
+        )
+
+    def merged_copy():
+        return remote(merged_sent, merged_got, merged_send, merged_recv, (row, mirror))
 
     def settle(ref, sem):
         pltpu.make_async_copy(ref, ref, sem).wait()
@@ -319,6 +323,7 @@
 
     early = 2 * slab_rows // 3
     late = slab_rows - slab_rows // 6
+    last = slab_rows - slab_rows // 12
 
     def one_row(s):
         settle(slot(slab, s), in_recv.at[s])
@@ -386,24 +391,38 @@
         s_hidden = (s_gate[...] * blended).astype(jnp.bfloat16)
         share = jnp.dot(s_hidden, single_out_ref[...], preferred_element_type=f32)
         for part in range(cols):
-            part_sent[part] = share[:, part * width : (part + 1) * width].astype(jnp.bfloat16)
-        for step in range(1, cols):
+            part_sent[part % near, (half + part // near) % 2] = share[
+                :, part * width : (part + 1) * width
+            ].astype(jnp.bfloat16)
+        for step in own_steps:
             part_copy(step).start()
 
-    @pl.loop(late, slab_rows)
+    @pl.loop(late, last)
     def _(s):
         send_row(s)
 
     with jax.named_scope('part'):
-        total = rest_ref[...].astype(f32) + part_sent[col].astype(f32)
-        settle(slot(part_got, others), part_recv)
-        for step in range(1, cols):
-            total = total + part_got[step].astype(f32)
-        single_new_ref[...] = total.astype(jnp.bfloat16)
+        nearby = pl.ds(0, near - 1)
+        settle(slot(part_got, nearby), part_recv)
+        merged = part_sent[lane, 1].astype(f32)
+        total = rest_ref[...].astype(f32) + part_sent[lane, 0].astype(f32)
+        for step in own_steps:
+            merged = merged + part_got[step, 1].astype(f32)
+            total = total + part_got[step, 0].astype(f32)
+        merged_sent[...] = merged.astype(jnp.bfloat16)
+        merged_copy().start()
+
+    @pl.loop(last, slab_rows)
+    def _(s):
+        send_row(s)
+
+    with jax.named_scope('merge'):
+        merged_copy().wait()
+        single_new_ref[...] = (total + merged_got[...].astype(f32)).astype(jnp.bfloat16)
 
     with jax.named_scope('drain'):
         settle(slot(head_sent, others), head_send)
-        settle(slot(part_sent, others), part_send)
+        settle(slot(part_sent, nearby), part_send)
         settle(slot(bands, row, others), col_send)
         settle(slot(bands, pl.ds(0, chips - 1)), chip_send)
         settle(slot(bands, pl.ds(0, chips)), core_send)
@@ -411,6 +430,32 @@
         settle(sent, in_send)
         settle(sent, out_send)
         settle(pair_out_ref, out_recv)
+
+
+def store_kernel(pair_ref, single_ref, pair_out_ref, single_out_ref, pair_sem, single_sem):
+    rows = pair_ref.shape[0]
+    chunks = math.gcd(rows, 8)
+    single = pltpu.make_async_copy(single_ref, single_out_ref, single_sem)
+    single.start()
+    for i in range(chunks):
+        span = pl.ds(i * (rows // chunks), rows // chunks)
+        pltpu.make_async_copy(pair_ref.at[span], pair_out_ref.at[span], pair_sem).start()
+    single.wait()
+    pltpu.make_async_copy(pair_ref, pair_out_ref, pair_sem).wait()
+
+
+def store(pair, single):
+    held = pl.BlockSpec(memory_space=pltpu.VMEM)
+    away = pl.BlockSpec(memory_space=pltpu.HBM)
+    return pl.pallas_call(
+        store_kernel,
+        in_specs=[held, held],
+        out_specs=[away, away],
+        out_shape=[jax.ShapeDtypeStruct(x.shape, x.dtype) for x in (pair, single)],
+        scratch_shapes=[pltpu.SemaphoreType.DMA, pltpu.SemaphoreType.DMA],
+        compiler_params=pltpu.CompilerParams(vmem_limit_bytes=4 * 2**20),
+        name="store",
+    )(*(pltpu.with_memory_space_constraint(x, pltpu.VMEM) for x in (pair, single)))
 
 
 def per_device(
@@ -480,8 +525,10 @@
             pltpu.VMEM((tokens, width), bf16),
             pltpu.VMEM((tokens, width), bf16),
             pltpu.VMEM((rows_here, width), f32),
-            pltpu.VMEM((cols, rows_here, width), bf16),
-            pltpu.VMEM((cols, rows_here, width), bf16),
+            pltpu.VMEM((cols // 2, 2, rows_here, width), bf16),
+            pltpu.VMEM((cols // 2, 2, rows_here, width), bf16),
+            pltpu.VMEM((rows_here, width), bf16),
+            pltpu.VMEM((rows_here, width), bf16),
             dma,
             dma((slab_rows,)),
             dma,
@@ -492,6 +539,8 @@
             dma((chips - 1,)),
             dma,
             dma((chips,)),
+            dma,
+            dma,
             dma,
             dma,
             dma,
@@ -505,7 +554,7 @@
         length, pair_rep, single_rep, pair_proj, pair_out_weight, single_proj_t, single_out_weight,
         pair_gain, bias_weight.T, bias_norm_gain, single_bias_weight.T, single_gain,
     )
-    return (pair_out, single_out)
+    return store(pair_out, single_out)
 
 
 def solution(mesh):

time: 122 us -> 121 us (level)
  local copies, waits for them, and re-layouts: 2.02 us -> 0 us
    unnamed x2 -> x0, local copies, waits for them, and re-layouts: 2.02 us -> none
    pallas_call x0 -> x1, Pallas kernels: none -> 1.42 us  [store(): pl.pallas_call(store_kernel, in_specs=[held, held], out_specs=[away, away...]
where the time goes in v2:
time: 121 us; the launch traced here: 120 us
  Pallas kernels  119 us (98%)
  between operations  1.29 us (1%)
    pallas_call x1, Pallas kernels, per_device(): pl.pallas_call(window_kernel, in_specs=[stay] * 12, out_specs=[anywhere,...  118 us

profile of v2, /device:TPU:0, one launch (start us, length us, event | category | flops | bytes accessed | tf_op | source)
XLA Modules:
  0.0 120.4 jit_solution(7732334654591404633)
XLA Ops:
  1.3 117.7 %window.1 = (bf16[48,96,256]{2,1,0:T(8,128)(2,1)S(1)}, bf16[48,192]{1,0:T(8,128)(2,1)S(1)}) custom-call(s32[1]{0:T(128)S(6)} %copy.14.length_hbm, bf16[48,96,256]{2,1,0:T(8,128)(2,1)} %pair_ref.1, bf16[384,768]{1,0:T(8,128)(2,1)} %single_hbm.1, bf16[4,256,256]{2,1,0:T(8,128)(2,1)} %proj_hbm.1, bf16[256,256]{1,0:T(8,128)(2,1)} %out_weight_hbm.1, ...), custom_call_target="tpu_custom_call" | custom-call | tf_op jit(solution)/shard_map/window/pallas_call | solution.py:490
  119.0 1.4 %store.1 = (bf16[48,96,256]{2,1,0:T(8,128)(2,1)}, bf16[48,192]{1,0:T(8,128)(2,1)}) custom-call(bf16[48,96,256]{2,1,0:T(8,128)(2,1)S(1)} %get-tuple-element.4.pair_ref, bf16[48,192]{1,0:T(8,128)(2,1)S(1)} %get-tuple-element.5.single_ref), custom_call_target="tpu_custom_call" | custom-call | tf_op jit(solution)/shard_map/store/pallas_call | solution.py:450

commit v3 on v2

--- a/solution.py
+++ b/solution.py
@@ -12,6 +12,7 @@
 SINGLE_HEAD_DIM = 48
 LOG2E = math.log2(math.e)
 
+LANES = 128
 masked_value = -1e30
 NT = (((1,), (1,)), ((), ()))
 
@@ -90,9 +91,11 @@
 ):
     f32 = jnp.float32
     slab_rows, cols, cols_here, channels = slab.shape
-    rows, _, heads, rows_here, _ = bands.shape
+    rows, _, bundles, rows_here, _ = bands.shape
+    heads_in = tri_kept.shape[0] // bundles
     tokens = cols * cols_here
     chips = rows // 2
+    s_heads = head_full.shape[0]
     row, col = lax.axis_index("row"), lax.axis_index("col")
     chip, core = row // 2, lax.rem(row, 2)
     partner = chip * 2 + 1 - core
@@ -248,7 +251,10 @@
                         preferred_element_type=f32,
                     )
 
-    tri_ref[...] = tri_kept[...].astype(jnp.bfloat16)
+    for bundle in range(bundles):
+        tri_ref[bundle] = jnp.concatenate(
+            [tri_kept[bundle * heads_in + i] for i in range(heads_in)], axis=1
+        ).astype(jnp.bfloat16)
     for step in (0, *own_steps):
         col_copy(step).start()
     own_block = pltpu.make_async_copy(tri_ref, slot(bands, row, col), col_recv.at[1])
@@ -303,13 +309,16 @@
         start = pl.multiple_of(band * rows_here, rows_here)
         for part in range(cols):
             usable = (
-                lax.broadcasted_iota(jnp.int32, (1, 1, cols_here), 2) + part * cols_here
+                lax.broadcasted_iota(jnp.int32, (1, cols_here), 1) + part * cols_here
                 < length_ref[0]
             )
-            piece = bands[band, part].astype(f32) * LOG2E
-            bias_held[:, pl.ds(start, rows_here), part * cols_here : (part + 1) * cols_here] = (
-                jnp.where(usable, piece, masked_value)
-            )
+            place = (pl.ds(start, rows_here), slice(part * cols_here, (part + 1) * cols_here))
+            for bundle in range(bundles):
+                piece = bands[band, part, bundle].astype(f32) * LOG2E
+                for i in range(heads_in):
+                    bias_held[bundle * heads_in + i, *place] = jnp.where(
+                        usable, piece[:, i * cols_here : (i + 1) * cols_here], masked_value
+                    )
 
     with jax.named_scope('bands'):
         take_band(row)
@@ -333,9 +342,10 @@
         )
         fresh[s] = updated.reshape(cols, cols_here, channels)
         again = normalize(updated, bias_gain_ref[...])
-        head_kept[:, s, :] = lax.dot_general(
-            head_weight_ref[...], again, NT, preferred_element_type=f32
-        )
+        found = lax.dot_general(head_weight_ref[...], again, NT, preferred_element_type=f32)
+        for head in range(found.shape[0]):
+            line = pl.ds(head % s_heads * slab_rows + s, 1)
+            head_kept[head // s_heads, line, :] = found[head : head + 1]
 
     def send_row(s):
         own_out(s).start()
@@ -351,7 +361,7 @@
             def _():
                 send_row(s)
 
-    head_sent[...] = head_kept[...].astype(jnp.bfloat16).reshape(head_sent.shape)
+    head_sent[...] = head_kept[...].astype(jnp.bfloat16)
     for step in range(1, cols):
         head_copy(step).start()
 
@@ -364,16 +374,20 @@
     for part in range(cols):
         span = slice(part * slab_rows, (part + 1) * slab_rows)
 
+        def fill_head(source):
+            block = source[part].astype(f32) * LOG2E
+            for head in range(s_heads):
+                head_full[head, span, :] = block[head * slab_rows : (head + 1) * slab_rows]
+
         @pl.when(col == part)
         def _():
-            head_full[:, span, :] = head_sent[part].astype(f32) * LOG2E
+            fill_head(head_sent)
 
         @pl.when(col != part)
         def _():
-            head_full[:, span, :] = head_got[part].astype(f32) * LOG2E
+            fill_head(head_got)
 
     with jax.named_scope('sattn'):
-        s_heads = head_full.shape[0]
         usable = lax.broadcasted_iota(jnp.int32, (1, tokens), 1) < length_ref[0]
         head_of_lane = lax.broadcasted_iota(jnp.int32, (1, width), 1) // SINGLE_HEAD_DIM
         blended = jnp.zeros((rows_here, width), f32)
@@ -478,6 +492,7 @@
     slab_rows = rows_here // cols
     chips = rows // 2
     heads = bias_weight.shape[1]
+    heads_in = math.gcd(heads, LANES // math.gcd(LANES, cols_here))
     single_heads = single_bias_weight.shape[1]
     heads_here = single_heads // cols
     width = single_proj.shape[2]
@@ -498,7 +513,7 @@
         scratch_shapes=[
             pltpu.VMEM(pair_rep.shape, bf16),
             pltpu.VMEM((heads, rows_here, cols_here), f32),
-            pltpu.VMEM((heads, rows_here, cols_here), bf16),
+            pltpu.VMEM((heads // heads_in, rows_here, heads_in * cols_here), bf16),
             pltpu.VMEM(single_rep.shape, bf16),
             pltpu.VMEM(pair_proj.shape, bf16),
             pltpu.VMEM(pair_out_weight.shape, bf16),
@@ -515,11 +530,11 @@
             dma((11,)),
             pltpu.VMEM((slab_rows, cols, cols_here, channels), bf16),
             pltpu.VMEM((slab_rows, cols, cols_here, channels), bf16),
-            pltpu.VMEM((rows, cols, heads, rows_here, cols_here), bf16),
+            pltpu.VMEM((rows, cols, heads // heads_in, rows_here, heads_in * cols_here), bf16),
             pltpu.VMEM((heads, tokens, tokens), f32),
-            pltpu.VMEM((single_heads, slab_rows, tokens), f32),
-            pltpu.VMEM((cols, heads_here, slab_rows, tokens), bf16),
-            pltpu.VMEM((cols, heads_here, slab_rows, tokens), bf16),
+            pltpu.VMEM((cols, heads_here * slab_rows, tokens), f32),
+            pltpu.VMEM((cols, heads_here * slab_rows, tokens), bf16),
+            pltpu.VMEM((cols, heads_here * slab_rows, tokens), bf16),
             pltpu.VMEM((heads_here, rows_here, tokens), f32),
             pltpu.VMEM((rows_here, width), bf16),
             pltpu.VMEM((tokens, width), bf16),

time: 121 us -> 118 us (0.975)
  Pallas kernels: 119 us -> 117 us
    pallas_call x1, Pallas kernels: 118 us -> 116 us  [per_device(): pl.pallas_call(window_kernel, in_specs=[stay] * 12, out_specs=[anywhere,...]
where the time goes in v3:
time: 118 us
  Pallas kernels  117 us (99%)
  between operations  1.29 us (1%)
    pallas_call x1, Pallas kernels, per_device(): pl.pallas_call(window_kernel, in_specs=[stay] * 12, out_specs=[anywhere,...  116 us

profile of v3, /device:TPU:0, one launch (start us, length us, event | category | flops | bytes accessed | tf_op | source)
XLA Modules:
  0.0 118.3 jit_solution(6533308808324935788)
XLA Ops:
  1.3 115.6 %window.1 = (bf16[48,96,256]{2,1,0:T(8,128)(2,1)S(1)}, bf16[48,192]{1,0:T(8,128)(2,1)S(1)}) custom-call(s32[1]{0:T(128)S(6)} %copy.14.length_hbm, bf16[48,96,256]{2,1,0:T(8,128)(2,1)} %pair_ref.1, bf16[384,768]{1,0:T(8,128)(2,1)} %single_hbm.1, bf16[4,256,256]{2,1,0:T(8,128)(2,1)} %proj_hbm.1, bf16[256,256]{1,0:T(8,128)(2,1)} %out_weight_hbm.1, ...), custom_call_target="tpu_custom_call" | custom-call | tf_op jit(solution)/shard_map/window/pallas_call | solution.py:505
  116.9 1.4 %store.1 = (bf16[48,96,256]{2,1,0:T(8,128)(2,1)}, bf16[48,192]{1,0:T(8,128)(2,1)}) custom-call(bf16[48,96,256]{2,1,0:T(8,128)(2,1)S(1)} %get-tuple-element.4.pair_ref, bf16[48,192]{1,0:T(8,128)(2,1)S(1)} %get-tuple-element.5.single_ref), custom_call_target="tpu_custom_call" | custom-call | tf_op jit(solution)/shard_map/store/pallas_call | solution.py:464

commit v4 on v3

--- a/solution.py
+++ b/solution.py
@@ -72,6 +72,41 @@
     ).astype(jnp.bfloat16)
 
 
+def folded(rows, width):
+    full, odd = width // LANES * LANES, width % LANES
+    if full and odd and 2 * odd == LANES:
+        return (rows * (full // LANES) + rows // 2, LANES)
+    return (rows, width)
+
+
+def fold(value, ref):
+    rows, width = value.shape
+    if ref.shape == value.shape:
+        ref[...] = value.astype(ref.dtype)
+        return
+    full = width // LANES
+    for i in range(full):
+        ref[i * rows : (i + 1) * rows] = value[:, i * LANES : (i + 1) * LANES].astype(ref.dtype)
+    odd = value[:, full * LANES :]
+    ref[full * rows :] = jnp.concatenate(
+        [odd[: rows // 2], odd[rows // 2 :]], axis=1
+    ).astype(ref.dtype)
+
+
+def unfold(ref, shape):
+    value = ref[...].astype(jnp.float32)
+    if ref.shape == shape:
+        return value
+    rows, width = shape
+    full = width // LANES
+    odd = value[full * rows :]
+    cut = width - full * LANES
+    pieces = [value[i * rows : (i + 1) * rows] for i in range(full)]
+    return jnp.concatenate(
+        pieces + [jnp.concatenate([odd[:, :cut], odd[:, cut:]], axis=0)], axis=1
+    )
+
+
 def slot(ref, *index):
     return ref.at[index]
 
@@ -84,10 +119,12 @@
     gain_ref, tri_weight_ref, bias_gain_ref, head_weight_ref, single_gain_ref, length_ref,
     rest_ref, local_sem, weight_sem,
     slab, fresh, bands, bias_held, head_kept, head_sent, head_got, head_full,
+    cross_kept, cross_sent, cross_got, early_kept, early_sent, early_got,
     s_query, s_key, s_value, s_gate, part_sent, part_got, merged_sent, merged_got,
     in_send, in_recv, out_send, out_recv,
     col_send, col_recv, chip_send, chip_recv, core_send, core_recv,
-    head_send, head_recv, part_send, part_recv, merged_send, merged_recv,
+    head_send, head_recv, cross_send, cross_recv, early_send, early_recv,
+    part_send, part_recv, merged_send, merged_recv,
 ):
     f32 = jnp.float32
     slab_rows, cols, cols_here, channels = slab.shape
@@ -194,26 +231,39 @@
             slot(pair_ref, col * slab_rows + s), slot(slab, s, col), in_recv.at[s]
         )
 
+    lane, half = lax.rem(col, near), col // near
+    early = 2 * slab_rows // 3
+
     def out_copy(s, step):
         to = peer(step)
+        kind = jnp.where(jnp.logical_and(to // near != half, s < early), 1 + s, 0)
         return remote(
             slot(fresh, s, to), slot(pair_out_ref, col * slab_rows + s),
-            out_send, out_recv, (row, to),
+            out_send, out_recv.at[kind], (row, to),
         )
 
     def own_out(s):
         return pltpu.make_async_copy(
-            slot(fresh, s, col), slot(pair_out_ref, col * slab_rows + s), out_recv
+            slot(fresh, s, col), slot(pair_out_ref, col * slab_rows + s), out_recv.at[0]
         )
 
     def head_copy(step):
-        to = peer(step)
+        to = near_peer(step)
+        return remote(slot(head_sent, to), slot(head_got, lane), head_send, head_recv, (row, to))
+
+    def cross_copy(step):
+        place = lax.rem(lane + step, near)
+        to = (1 - half) * near + place
         return remote(
-            slot(head_sent, to), slot(head_got, col), head_send, head_recv,
-            (row, to),
-        )
-
-    lane, half = lax.rem(col, near), col // near
+            slot(cross_sent, place), slot(cross_got, lane), cross_send, cross_recv, (row, to)
+        )
+
+    def early_copy(step):
+        to = near_peer(step)
+        return remote(
+            slot(early_sent, lax.rem(to, near)), slot(early_got, lane),
+            early_send, early_recv, (row, to),
+        )
 
     def part_copy(step):
         return remote(
@@ -330,7 +380,7 @@
             core_copy(step).wait_recv()
             take_band(chip_back(step) + 1 - 2 * core)
 
-    early = 2 * slab_rows // 3
+    middle = early + slab_rows // 12
     late = slab_rows - slab_rows // 6
     last = slab_rows - slab_rows // 12
 
@@ -362,30 +412,94 @@
                 send_row(s)
 
     head_sent[...] = head_kept[...].astype(jnp.bfloat16)
-    for step in range(1, cols):
+    wide = near * cols_here
+    rest = slab_rows - early
+    top_heads = s_heads // 2
+    for part in range(cols):
+        mine = slice((1 - part // near) * wide, (2 - part // near) * wide)
+
+        @pl.when(half != part // near)
+        def _():
+            for head in range(s_heads):
+                begin = head * slab_rows
+                up = head % top_heads * early
+                side = head // top_heads * wide
+                cross_kept[up : up + early, side : side + wide] = head_kept[
+                    part, begin : begin + early, mine
+                ]
+                down = top_heads * early + head * rest
+                cross_kept[down : down + rest, :] = head_kept[
+                    part, begin + early : begin + slab_rows, :
+                ]
+            cross_sent[part % near] = cross_kept[...].astype(jnp.bfloat16)
+
+    for step in range(near):
+        cross_copy(step).start()
+    for step in own_steps:
         head_copy(step).start()
-
-    @pl.loop(early, late)
+    head_got[lane] = head_sent[col]
+
+    @pl.loop(early, middle)
     def _(s):
         send_row(s)
 
+    with jax.named_scope('recompute'):
+
+        @pl.loop(0, early)
+        def _(s):
+            settle(slot(pair_out_ref, pl.ds(0, near)), out_recv.at[1 + s])
+            for other in range(near):
+                line = ((1 - half) * near + other) * slab_rows + s
+                again = normalize(pair_out_ref[line], bias_gain_ref[...])
+                found = lax.dot_general(head_weight_ref[...], again, NT, preferred_element_type=f32)
+                for head in range(found.shape[0]):
+                    at = (head % s_heads * near + other) * early + s
+                    early_kept[head // s_heads, pl.ds(at, 1), :] = found[head : head + 1]
+
+        for place in range(near):
+            early_sent[place] = early_kept[half * near + place].astype(jnp.bfloat16)
+        for step in own_steps:
+            early_copy(step).start()
+        early_got[lane] = early_sent[lane]
+
+    @pl.loop(middle, late)
+    def _(s):
+        send_row(s)
+
+    nearby = pl.ds(0, near - 1)
     with jax.named_scope('headwait'):
-        settle(slot(head_got, others), head_recv)
+        settle(slot(head_got, nearby), head_recv)
+        settle(cross_got, cross_recv)
+        settle(slot(early_got, nearby), early_recv)
     for part in range(cols):
-        span = slice(part * slab_rows, (part + 1) * slab_rows)
-
-        def fill_head(source):
-            block = source[part].astype(f32) * LOG2E
+        first = part * slab_rows
+        place, side = part % near, part // near
+
+        @pl.when(half == side)
+        def _():
+            block = head_got[place].astype(f32) * LOG2E
             for head in range(s_heads):
-                head_full[head, span, :] = block[head * slab_rows : (head + 1) * slab_rows]
-
-        @pl.when(col == part)
+                head_full[head, first : first + slab_rows, :] = block[
+                    head * slab_rows : (head + 1) * slab_rows
+                ]
+
+        @pl.when(half != side)
         def _():
-            fill_head(head_sent)
-
-        @pl.when(col != part)
-        def _():
-            fill_head(head_got)
+            block = cross_got[place].astype(f32) * LOG2E
+            for head in range(s_heads):
+                up = head % top_heads * early
+                from_side = head // top_heads * wide
+                head_full[head, first : first + early, side * wide : (side + 1) * wide] = block[
+                    up : up + early, from_side : from_side + wide
+                ]
+                down = top_heads * early + head * rest
+                head_full[head, first + early : first + slab_rows, :] = block[down : down + rest]
+                at = (head * near + place) * early
+                for source in range(near):
+                    begin = ((1 - side) * near + source) * cols_here
+                    head_full[head, first : first + early, begin : begin + cols_here] = (
+                        early_got[source, at : at + early, :].astype(f32) * LOG2E
+                    )
 
     with jax.named_scope('sattn'):
         usable = lax.broadcasted_iota(jnp.int32, (1, tokens), 1) < length_ref[0]
@@ -416,14 +530,13 @@
         send_row(s)
 
     with jax.named_scope('part'):
-        nearby = pl.ds(0, near - 1)
         settle(slot(part_got, nearby), part_recv)
         merged = part_sent[lane, 1].astype(f32)
         total = rest_ref[...].astype(f32) + part_sent[lane, 0].astype(f32)
         for step in own_steps:
             merged = merged + part_got[step, 1].astype(f32)
             total = total + part_got[step, 0].astype(f32)
-        merged_sent[...] = merged.astype(jnp.bfloat16)
+        fold(merged, merged_sent)
         merged_copy().start()
 
     @pl.loop(last, slab_rows)
@@ -432,10 +545,12 @@
 
     with jax.named_scope('merge'):
         merged_copy().wait()
-        single_new_ref[...] = (total + merged_got[...].astype(f32)).astype(jnp.bfloat16)
+        single_new_ref[...] = (total + unfold(merged_got, total.shape)).astype(jnp.bfloat16)
 
     with jax.named_scope('drain'):
-        settle(slot(head_sent, others), head_send)
+        settle(slot(head_sent, nearby), head_send)
+        settle(cross_sent, cross_send)
+        settle(slot(early_sent, nearby), early_send)
         settle(slot(part_sent, nearby), part_send)
         settle(slot(bands, row, others), col_send)
         settle(slot(bands, pl.ds(0, chips - 1)), chip_send)
@@ -443,7 +558,7 @@
         sent = slot(local, pl.ds(0, slab_rows * (cols - 1)))
         settle(sent, in_send)
         settle(sent, out_send)
-        settle(pair_out_ref, out_recv)
+        settle(slot(pair_out_ref, pl.ds(0, rows_here - near * early)), out_recv.at[0])
 
 
 def store_kernel(pair_ref, single_ref, pair_out_ref, single_out_ref, pair_sem, single_sem):
@@ -496,6 +611,9 @@
     single_heads = single_bias_weight.shape[1]
     heads_here = single_heads // cols
     width = single_proj.shape[2]
+    near = cols // 2
+    early = 2 * slab_rows // 3
+    cross_rows = heads_here // 2 * early + heads_here * (slab_rows - early)
     single_proj_t = single_proj.transpose(0, 2, 1)
     bf16, f32 = jnp.bfloat16, jnp.float32
     dma = pltpu.SemaphoreType.DMA
@@ -505,7 +623,7 @@
     pair_out, single_out = pl.pallas_call(
         window_kernel,
         in_specs=[stay] * 12,
-        out_specs=[anywhere, held],
+        out_specs=[held, held],
         out_shape=[
             pltpu.VMEM(pair_rep.shape, bf16),
             pltpu.VMEM((rows_here, width), bf16),
@@ -534,26 +652,36 @@
             pltpu.VMEM((heads, tokens, tokens), f32),
             pltpu.VMEM((cols, heads_here * slab_rows, tokens), f32),
             pltpu.VMEM((cols, heads_here * slab_rows, tokens), bf16),
-            pltpu.VMEM((cols, heads_here * slab_rows, tokens), bf16),
+            pltpu.VMEM((near, heads_here * slab_rows, tokens), bf16),
             pltpu.VMEM((heads_here, rows_here, tokens), f32),
+            pltpu.VMEM((cross_rows, tokens), f32),
+            pltpu.VMEM((near, cross_rows, tokens), bf16),
+            pltpu.VMEM((near, cross_rows, tokens), bf16),
+            pltpu.VMEM((cols, heads_here * near * early, cols_here), f32),
+            pltpu.VMEM((near, heads_here * near * early, cols_here), bf16),
+            pltpu.VMEM((near, heads_here * near * early, cols_here), bf16),
             pltpu.VMEM((rows_here, width), bf16),
             pltpu.VMEM((tokens, width), bf16),
             pltpu.VMEM((tokens, width), bf16),
             pltpu.VMEM((rows_here, width), f32),
             pltpu.VMEM((cols // 2, 2, rows_here, width), bf16),
             pltpu.VMEM((cols // 2, 2, rows_here, width), bf16),
-            pltpu.VMEM((rows_here, width), bf16),
-            pltpu.VMEM((rows_here, width), bf16),
+            pltpu.VMEM(folded(rows_here, width), bf16),
+            pltpu.VMEM(folded(rows_here, width), bf16),
             dma,
             dma((slab_rows,)),
             dma,
-            dma,
+            dma((1 + early,)),
             dma,
             dma((2,)),
             dma,
             dma((chips - 1,)),
             dma,
             dma((chips,)),
+            dma,
+            dma,
+            dma,
+            dma,
             dma,
             dma,
             dma,

time: 118 us -> 117 us (level)
    pallas_call x1, Pallas kernels: 116 us -> 114 us  [per_device(): pl.pallas_call(window_kernel, in_specs=[stay] * 12, out_specs=[held, held...]
where the time goes in v4:
time: 117 us
  Pallas kernels  116 us (99%)
  between operations  1.29 us (1%)
    pallas_call x1, Pallas kernels, per_device(): pl.pallas_call(window_kernel, in_specs=[stay] * 12, out_specs=[held, held...  114 us

profile of v4, /device:TPU:0, one launch (start us, length us, event | category | flops | bytes accessed | tf_op | source)
XLA Modules:
  0.0 117.1 jit_solution(6544716359989721649)
XLA Ops:
  1.3 114.4 %window.1 = (bf16[48,96,256]{2,1,0:T(8,128)(2,1)S(1)}, bf16[48,192]{1,0:T(8,128)(2,1)S(1)}) custom-call(s32[1]{0:T(128)S(6)} %copy.14.length_hbm, bf16[48,96,256]{2,1,0:T(8,128)(2,1)} %pair_ref.1, bf16[384,768]{1,0:T(8,128)(2,1)} %single_hbm.1, bf16[4,256,256]{2,1,0:T(8,128)(2,1)} %proj_hbm.1, bf16[256,256]{1,0:T(8,128)(2,1)} %out_weight_hbm.1, ...), custom_call_target="tpu_custom_call" | custom-call | tf_op jit(solution)/shard_map/window/pallas_call | solution.py:623
  115.7 1.4 %store.1 = (bf16[48,96,256]{2,1,0:T(8,128)(2,1)}, bf16[48,192]{1,0:T(8,128)(2,1)}) custom-call(bf16[48,96,256]{2,1,0:T(8,128)(2,1)S(1)} %get-tuple-element.4.pair_ref, bf16[48,192]{1,0:T(8,128)(2,1)S(1)} %get-tuple-element.5.single_ref), custom_call_target="tpu_custom_call" | custom-call | tf_op jit(solution)/shard_map/store/pallas_call | solution.py:579

commit v5 on v4

--- a/solution.py
+++ b/solution.py
@@ -124,7 +124,7 @@
     in_send, in_recv, out_send, out_recv,
     col_send, col_recv, chip_send, chip_recv, core_send, core_recv,
     head_send, head_recv, cross_send, cross_recv, early_send, early_recv,
-    part_send, part_recv, merged_send, merged_recv,
+    part_send, part_recv, merged_send, merged_recv, opened, met, entered,
 ):
     f32 = jnp.float32
     slab_rows, cols, cols_here, channels = slab.shape
@@ -170,11 +170,33 @@
         )
     ]
     barrier = pltpu.get_barrier_semaphore()
+    left, right = cols // 2 - 1, cols // 2
+    inner = jnp.logical_or(col == left, col == right)
+    outer = jnp.logical_not(inner)
+    guide = jnp.logical_or(col == 0, col == cols - 1)
+    follower = jnp.where(col == 0, left, right)
+    pair = cols - 1 - col
+
+    def signal(sem, to_row, to_col):
+        pl.semaphore_signal(sem, inc=1, device_id=(to_row, to_col), device_id_type=mesh_id)
+
+    def signal_rows(sem):
+        for step in range(1, chips):
+            signal(sem, chip_row(step), col)
+        signal(sem, partner, col)
+
     for step in range(1, cols):
-        pl.semaphore_signal(barrier, inc=1, device_id=(row, peer(step)), device_id_type=mesh_id)
-    for step in range(1, chips):
-        pl.semaphore_signal(barrier, inc=1, device_id=(chip_row(step), col), device_id_type=mesh_id)
-    pl.semaphore_signal(barrier, inc=1, device_id=(partner, col), device_id_type=mesh_id)
+        to = peer(step)
+        to_outer = jnp.logical_and(to != left, to != right)
+
+        @pl.when(jnp.logical_or(to_outer, jnp.logical_and(inner, to == pair)))
+        def _():
+            signal(barrier, row, to)
+
+    @pl.when(outer)
+    def _():
+        signal_rows(barrier)
+
     for copy in weight_copies[:2]:
         copy.start()
     for part in range(cols):
@@ -182,7 +204,18 @@
     for copy in weight_copies[2:]:
         copy.start()
     with jax.named_scope('bar'):
-        pl.semaphore_wait(barrier, cols + chips - 1)
+        @pl.when(inner)
+        def _():
+            pl.semaphore_wait(barrier, 1)
+
+        @pl.when(outer)
+        def _():
+            pl.semaphore_wait(barrier, cols + chips - 1)
+
+    @pl.when(guide)
+    def _():
+        signal(opened, row, follower)
+        signal_rows(met)
 
     def remote(src, dst, send, recv, to):
         return pltpu.make_async_remote_copy(
@@ -219,8 +252,7 @@
             (partner, col),
         )
 
-    def in_copy(s, step):
-        to = peer(step)
+    def in_copy(s, to):
         return remote(
             slot(pair_ref, to * slab_rows + s), slot(slab, s, col),
             in_send, in_recv.at[s], (row, to),
@@ -282,9 +314,27 @@
     def bring_row(s):
         own_in(s).start()
         for step in range(1, cols):
-            in_copy(s, step).start()
-
-    bring_row(0)
+            in_copy(s, peer(step)).start()
+
+    def bring_rest(s):
+        own_in(s).start()
+        for step in range(1, cols):
+
+            @pl.when(peer(step) != pair)
+            def _():
+                in_copy(s, peer(step)).start()
+
+    first_rows = min(2, slab_rows)
+
+    @pl.when(inner)
+    def _():
+        for s in range(first_rows):
+            in_copy(s, pair).start()
+
+    @pl.when(outer)
+    def _():
+        bring_row(0)
+
     for copy in weight_copies[:2]:
         copy.wait()
     with jax.named_scope('tri'):
@@ -305,14 +355,35 @@
         tri_ref[bundle] = jnp.concatenate(
             [tri_kept[bundle * heads_in + i] for i in range(heads_in)], axis=1
         ).astype(jnp.bfloat16)
+    @pl.when(inner)
+    def _():
+        pl.semaphore_wait(opened, 1)
+
     for step in (0, *own_steps):
         col_copy(step).start()
     own_block = pltpu.make_async_copy(tri_ref, slot(bands, row, col), col_recv.at[1])
     own_block.start()
 
     ahead = min(3, slab_rows)
-    for s in range(1, ahead):
+
+    @pl.when(inner)
+    def _():
+        for s in range(first_rows):
+            bring_rest(s)
+
+    @pl.when(outer)
+    def _():
+        for s in range(1, first_rows):
+            bring_row(s)
+
+    for s in range(first_rows, ahead):
         bring_row(s)
+
+    @pl.when(guide)
+    def _():
+        pl.semaphore_wait(met, chips)
+        signal(entered, row, follower)
+
     with jax.named_scope('waitmirror'):
         col_copy(0).wait_recv()
     for step in mirror_steps:
@@ -327,6 +398,10 @@
 
     with jax.named_scope('waitcols'):
         settle(slot(bands, row, others), col_recv.at[1])
+    @pl.when(inner)
+    def _():
+        pl.semaphore_wait(entered, 1)
+
     for step in range(1, chips):
         chip_copy(step).start()
     core_copy(0).start()
@@ -688,6 +763,9 @@
             dma,
             dma,
             dma,
+            pltpu.SemaphoreType.REGULAR,
+            pltpu.SemaphoreType.REGULAR,
+            pltpu.SemaphoreType.REGULAR,
         ],
         compiler_params=pltpu.CompilerParams(
             collective_id=0, has_side_effects=True, vmem_limit_bytes=56 * 2**20

time: 117 us -> 116 us (level)
  no operation moved by 1% of the time
where the time goes in v5:
time: 116 us
  Pallas kernels  115 us (99%)
  between operations  1.29 us (1%)
    pallas_call x1, Pallas kernels, per_device(): pl.pallas_call(window_kernel, in_specs=[stay] * 12, out_specs=[held, held...  113 us

profile of v5, /device:TPU:0, one launch (start us, length us, event | category | flops | bytes accessed | tf_op | source)
XLA Modules:
  0.0 116.1 jit_solution(13428769036911085914)
XLA Ops:
  1.3 113.4 %window.1 = (bf16[48,96,256]{2,1,0:T(8,128)(2,1)S(1)}, bf16[48,192]{1,0:T(8,128)(2,1)S(1)}) custom-call(s32[1]{0:T(128)S(6)} %copy.14.length_hbm, bf16[48,96,256]{2,1,0:T(8,128)(2,1)} %pair_ref.1, bf16[384,768]{1,0:T(8,128)(2,1)} %single_hbm.1, bf16[4,256,256]{2,1,0:T(8,128)(2,1)} %proj_hbm.1, bf16[256,256]{1,0:T(8,128)(2,1)} %out_weight_hbm.1, ...), custom_call_target="tpu_custom_call" | custom-call | tf_op jit(solution)/shard_map/window/pallas_call | solution.py:698
  114.7 1.4 %store.1 = (bf16[48,96,256]{2,1,0:T(8,128)(2,1)}, bf16[48,192]{1,0:T(8,128)(2,1)}) custom-call(bf16[48,96,256]{2,1,0:T(8,128)(2,1)S(1)} %get-tuple-element.4.pair_ref, bf16[48,192]{1,0:T(8,128)(2,1)S(1)} %get-tuple-element.5.single_ref), custom_call_target="tpu_custom_call" | custom-call | tf_op jit(solution)/shard_map/store/pallas_call | solution.py:654

commit v6 on v5

--- a/solution.py
+++ b/solution.py
@@ -472,6 +472,14 @@
             line = pl.ds(head % s_heads * slab_rows + s, 1)
             head_kept[head // s_heads, line, :] = found[head : head + 1]
 
+    def send_part(s, to_inner):
+        for step in range(1, cols):
+            to = peer(step)
+
+            @pl.when(jnp.logical_or(to == left, to == right) == to_inner)
+            def _():
+                out_copy(s, step).start()
+
     def send_row(s):
         own_out(s).start()
         for step in range(1, cols):
@@ -600,9 +608,14 @@
         for step in own_steps:
             part_copy(step).start()
 
+    @pl.loop(late, slab_rows)
+    def _(s):
+        own_out(s).start()
+        send_part(s, False)
+
     @pl.loop(late, last)
     def _(s):
-        send_row(s)
+        send_part(s, True)
 
     with jax.named_scope('part'):
         settle(slot(part_got, nearby), part_recv)
@@ -616,7 +629,7 @@
 
     @pl.loop(last, slab_rows)
     def _(s):
-        send_row(s)
+        send_part(s, True)
 
     with jax.named_scope('merge'):
         merged_copy().wait()

time: 116 us -> 116 us (level)
  no operation moved by 1% of the time
where the time goes in v6:
time: 116 us; the launch traced here: 115 us
  Pallas kernels  114 us (98%)
  between operations  1.29 us (1%)
    pallas_call x1, Pallas kernels, per_device(): pl.pallas_call(window_kernel, in_specs=[stay] * 12, out_specs=[held, held...  113 us

profile of v6, /device:TPU:0, one launch (start us, length us, event | category | flops | bytes accessed | tf_op | source)
XLA Modules:
  0.0 115.5 jit_solution(15621046324472473035)
XLA Ops:
  1.3 112.8 %window.1 = (bf16[48,96,256]{2,1,0:T(8,128)(2,1)S(1)}, bf16[48,192]{1,0:T(8,128)(2,1)S(1)}) custom-call(s32[1]{0:T(128)S(6)} %copy.14.length_hbm, bf16[48,96,256]{2,1,0:T(8,128)(2,1)} %pair_ref.1, bf16[384,768]{1,0:T(8,128)(2,1)} %single_hbm.1, bf16[4,256,256]{2,1,0:T(8,128)(2,1)} %proj_hbm.1, bf16[256,256]{1,0:T(8,128)(2,1)} %out_weight_hbm.1, ...), custom_call_target="tpu_custom_call" | custom-call | tf_op jit(solution)/shard_map/window/pallas_call | solution.py:711
  114.1 1.4 %store.1 = (bf16[48,96,256]{2,1,0:T(8,128)(2,1)}, bf16[48,192]{1,0:T(8,128)(2,1)}) custom-call(bf16[48,96,256]{2,1,0:T(8,128)(2,1)S(1)} %get-tuple-element.4.pair_ref, bf16[48,192]{1,0:T(8,128)(2,1)S(1)} %get-tuple-element.5.single_ref), custom_call_target="tpu_custom_call" | custom-call | tf_op jit(solution)/shard_map/store/pallas_call | solution.py:667

commit v7 on v6

--- a/solution.py
+++ b/solution.py
@@ -613,9 +613,11 @@
         own_out(s).start()
         send_part(s, False)
 
-    @pl.loop(late, last)
-    def _(s):
-        send_part(s, True)
+    @pl.when(outer)
+    def _():
+        @pl.loop(late, last)
+        def _(s):
+            send_part(s, True)
 
     with jax.named_scope('part'):
         settle(slot(part_got, nearby), part_recv)
@@ -626,6 +628,12 @@
             total = total + part_got[step, 0].astype(f32)
         fold(merged, merged_sent)
         merged_copy().start()
+
+    @pl.when(inner)
+    def _():
+        @pl.loop(late, last)
+        def _(s):
+            send_part(s, True)
 
     @pl.loop(last, slab_rows)
     def _(s):

time: 116 us -> 115 us (level)
  no operation moved by 1% of the time
where the time goes in v7:
time: 115 us; the launch traced here: 114 us
  Pallas kernels  113 us (98%)
  between operations  1.29 us (1%)
    pallas_call x1, Pallas kernels, per_device(): pl.pallas_call(window_kernel, in_specs=[stay] * 12, out_specs=[held, held...  112 us

profile of v7, /device:TPU:0, one launch (start us, length us, event | category | flops | bytes accessed | tf_op | source)
XLA Modules:
  0.0 114.4 jit_solution(4412176609220582261)
XLA Ops:
  1.3 111.7 %window.1 = (bf16[48,96,256]{2,1,0:T(8,128)(2,1)S(1)}, bf16[48,192]{1,0:T(8,128)(2,1)S(1)}) custom-call(s32[1]{0:T(128)S(6)} %copy.14.length_hbm, bf16[48,96,256]{2,1,0:T(8,128)(2,1)} %pair_ref.1, bf16[384,768]{1,0:T(8,128)(2,1)} %single_hbm.1, bf16[4,256,256]{2,1,0:T(8,128)(2,1)} %proj_hbm.1, bf16[256,256]{1,0:T(8,128)(2,1)} %out_weight_hbm.1, ...), custom_call_target="tpu_custom_call" | custom-call | tf_op jit(solution)/shard_map/window/pallas_call | solution.py:719
  113.0 1.4 %store.1 = (bf16[48,96,256]{2,1,0:T(8,128)(2,1)}, bf16[48,192]{1,0:T(8,128)(2,1)}) custom-call(bf16[48,96,256]{2,1,0:T(8,128)(2,1)S(1)} %get-tuple-element.4.pair_ref, bf16[48,192]{1,0:T(8,128)(2,1)S(1)} %get-tuple-element.5.single_ref), custom_call_target="tpu_custom_call" | custom-call | tf_op jit(solution)/shard_map/store/pallas_call | solution.py:675

commit v8 on v7

--- a/solution.py
+++ b/solution.py
@@ -133,6 +133,7 @@
     tokens = cols * cols_here
     chips = rows // 2
     s_heads = head_full.shape[0]
+    batch = slab_rows // in_recv.shape[0]
     row, col = lax.axis_index("row"), lax.axis_index("col")
     chip, core = row // 2, lax.rem(row, 2)
     partner = chip * 2 + 1 - core
@@ -255,12 +256,12 @@
     def in_copy(s, to):
         return remote(
             slot(pair_ref, to * slab_rows + s), slot(slab, s, col),
-            in_send, in_recv.at[s], (row, to),
+            in_send, in_recv.at[s // batch], (row, to),
         )
 
     def own_in(s):
         return pltpu.make_async_copy(
-            slot(pair_ref, col * slab_rows + s), slot(slab, s, col), in_recv.at[s]
+            slot(pair_ref, col * slab_rows + s), slot(slab, s, col), in_recv.at[s // batch]
         )
 
     lane, half = lax.rem(col, near), col // near
@@ -460,7 +461,10 @@
     last = slab_rows - slab_rows // 12
 
     def one_row(s):
-        settle(slot(slab, s), in_recv.at[s])
+        @pl.when(lax.rem(s, batch) == 0)
+        def _():
+            settle(slot(slab, pl.ds(s, batch)), in_recv.at[s // batch])
+
         rep = slab[s].reshape(tokens, channels)
         updated = row_update(
             rep, gain_ref[...], proj_ref, out_weight_ref[...], lambda head: bias_held[head]
@@ -765,7 +769,7 @@
             pltpu.VMEM(folded(rows_here, width), bf16),
             pltpu.VMEM(folded(rows_here, width), bf16),
             dma,
-            dma((slab_rows,)),
+            dma((slab_rows // math.gcd(slab_rows, 3),)),
             dma,
             dma((1 + early,)),
             dma,

time: 115 us -> 115 us (level)
  no operation moved by 1% of the time
where the time goes in v8:
time: 115 us; the launch traced here: 114 us
  Pallas kernels  113 us (98%)
  between operations  1.29 us (1%)
    pallas_call x1, Pallas kernels, per_device(): pl.pallas_call(window_kernel, in_specs=[stay] * 12, out_specs=[held, held...  112 us

profile of v8, /device:TPU:0, one launch (start us, length us, event | category | flops | bytes accessed | tf_op | source)
XLA Modules:
  0.0 114.4 jit_solution(5795592652830666537)
XLA Ops:
  1.3 111.7 %window.1 = (bf16[48,96,256]{2,1,0:T(8,128)(2,1)S(1)}, bf16[48,192]{1,0:T(8,128)(2,1)S(1)}) custom-call(s32[1]{0:T(128)S(6)} %copy.14.length_hbm, bf16[48,96,256]{2,1,0:T(8,128)(2,1)} %pair_ref.1, bf16[384,768]{1,0:T(8,128)(2,1)} %single_hbm.1, bf16[4,256,256]{2,1,0:T(8,128)(2,1)} %proj_hbm.1, bf16[256,256]{1,0:T(8,128)(2,1)} %out_weight_hbm.1, ...), custom_call_target="tpu_custom_call" | custom-call | tf_op jit(solution)/shard_map/window/pallas_call | solution.py:723
  112.9 1.4 %store.1 = (bf16[48,96,256]{2,1,0:T(8,128)(2,1)}, bf16[48,192]{1,0:T(8,128)(2,1)}) custom-call(bf16[48,96,256]{2,1,0:T(8,128)(2,1)S(1)} %get-tuple-element.4.pair_ref, bf16[48,192]{1,0:T(8,128)(2,1)S(1)} %get-tuple-element.5.single_ref), custom_call_target="tpu_custom_call" | custom-call | tf_op jit(solution)/shard_map/store/pallas_call | solution.py:679
